TPU v7x, 128 devices: a whole 4x4x4 slice. The times are simulated.
128 devices in a mesh: dp: 4 (over y), dict: 32 (over x, z, core).
Axes of the slice: x: 4, y: 4, z: 4, core: 2. Of those that a mesh axis runs over, the one named last changes fastest.
Arguments:
- acts: bfloat16 [8192, 8192], P('dict', 'dp'), may hold values from -6 to 6
- lists: int32 [512, 2], P('dict'), may hold values from 0 to 31, all different within a row; in each aligned block of 16 rows (0 to 15, 16 to 31, ...) at most 2 rows name the same one
- w_enc: bfloat16 [8192, 32768], P('dp', 'dict'), may hold values from -0.0625 to 0.0625
- w_dec: bfloat16 [32768, 8192], P('dict', 'dp'), may hold values from -0.1875 to 0.1875
- b_enc: bfloat16 [32768], P('dict'), may hold values from -3 to 3
- b_dec: bfloat16 [8192], P('dp'), may hold values from -3 to 3
Outputs:
- grad_enc: bfloat16 [8192, 32768], P('dp', 'dict')
- grad_dec: bfloat16 [32768, 8192], P('dict', 'dp')
Inputs may be any that keep to these rules, and one draw needn't show every extreme that they name: Each row block lists 2 different panels. Among the 16 row blocks of one index of dict, no panel is listed by more than 2 blocks, and some panel is listed by exactly 2.
All inputs are finite; a program needn't handle non-finite values.
Results may differ from a plain program's by a relative error of at most 0.0057.
Values may be sent and summed in bfloat16 or wider, within the bound.
No kernel may reach another device: no remote copies, remote signals or barrier semaphores. Data moves between devices by JAX's collectives and lax.ppermute only.
A program may use at most 128 MiB of HBM per device.

v0:
```python
import jax
import jax.numpy as jnp
from jax import lax
from jax.sharding import PartitionSpec as P


def on_device(acts, lists, w_enc, w_dec, b_enc, b_dec):
    peers = lax.axis_size("dict")
    block_count = lists.shape[0]
    active_count = lists.shape[1]
    rows_block = acts.shape[0] // block_count
    feature_cols = acts.shape[1]
    capacity = max(2, (2 * block_count * active_count + peers - 1) // peers)
    slot_total = peers * capacity
    flat_ids = lists.reshape(-1)
    onehot = (flat_ids[:, None] == jnp.arange(peers, dtype=jnp.int32)[None, :]).astype(jnp.int32)
    rank_index = jnp.sum((jnp.cumsum(onehot, axis=0) - 1) * onehot, axis=1)
    slot_index = flat_ids * capacity + rank_index
    item_block = jnp.arange(block_count * active_count, dtype=jnp.int32) // active_count
    slot_match = (jnp.arange(slot_total, dtype=jnp.int32)[:, None] == slot_index[None, :]).astype(
        jnp.float32
    )
    block_match = (item_block[:, None] == jnp.arange(block_count, dtype=jnp.int32)[None, :]).astype(
        jnp.float32
    )
    selector = jnp.dot(slot_match, block_match).astype(jnp.bfloat16)
    block_rows = acts.reshape(block_count, rows_block * feature_cols)
    outgoing = jnp.dot(selector, block_rows, preferred_element_type=jnp.float32).astype(
        jnp.bfloat16
    )
    outgoing = outgoing.reshape(peers, capacity * rows_block, feature_cols)
    received = lax.all_to_all(outgoing, "dict", split_axis=0, concat_axis=0, tiled=True)
    rows_in = received.reshape(-1, feature_cols)
    pre_local = jnp.dot(rows_in, w_enc, preferred_element_type=jnp.float32)
    bias_enc = b_enc.astype(jnp.float32)
    preact = lax.psum(pre_local, "dp") + bias_enc
    activity = (jnp.maximum(preact, 0.0) ** 2).astype(jnp.bfloat16)
    part = jnp.dot(activity, w_dec, preferred_element_type=jnp.float32).astype(jnp.bfloat16)
    part = part.reshape(peers, capacity * rows_block, feature_cols)
    returned = lax.all_to_all(part, "dict", split_axis=0, concat_axis=0, tiled=True)
    returned = returned.reshape(slot_total, rows_block * feature_cols)
    rebuilt = lax.dot_general(
        selector, returned, (((0,), (0,)), ((), ())), preferred_element_type=jnp.float32
    )
    rebuilt = rebuilt.reshape(block_count * rows_block, feature_cols) + b_dec.astype(jnp.float32)
    residual_g = ((rebuilt - acts.astype(jnp.float32)) * (1.0 / rows_block)).astype(jnp.bfloat16)
    resid_out = jnp.dot(
        selector,
        residual_g.reshape(block_count, rows_block * feature_cols),
        preferred_element_type=jnp.float32,
    ).astype(jnp.bfloat16)
    resid_out = resid_out.reshape(peers, capacity * rows_block, feature_cols)
    residual_in = lax.all_to_all(
        resid_out, "dict", split_axis=0, concat_axis=0, tiled=True
    ).reshape(-1, feature_cols)
    grad_dec = lax.dot_general(
        activity, residual_in, (((0,), (0,)), ((), ())), preferred_element_type=jnp.float32
    ).astype(jnp.bfloat16)
    dact_local = lax.dot_general(
        residual_in, w_dec, (((1,), (1,)), ((), ())), preferred_element_type=jnp.float32
    )
    dact = lax.psum(dact_local, "dp")
    grad_pre = (dact * 2.0 * jnp.maximum(preact, 0.0)).astype(jnp.bfloat16)
    grad_enc = lax.dot_general(
        rows_in, grad_pre, (((0,), (0,)), ((), ())), preferred_element_type=jnp.float32
    ).astype(jnp.bfloat16)
    return (grad_enc, grad_dec)


def solution(mesh):
    in_specs = (
        P("dict", "dp"),
        P("dict", None),
        P("dp", "dict"),
        P("dict", "dp"),
        P("dict"),
        P("dp"),
    )
    out_specs = (P("dp", "dict"), P("dict", "dp"))
    return jax.shard_map(
        on_device, mesh=mesh, in_specs=in_specs, out_specs=out_specs, check_vma=False
    )
```

profile of v0, /device:TPU:1, one launch (start us, length us, event | category | flops | bytes accessed | tf_op | source)
XLA Modules:
  0.0 449.6 jit_solution(6548300190928002087)
XLA Ops:
  7.2 0.0 all-reduce.3.cloned.1.call-start
  7.2 0.8 copy.9
  8.0 0.1 reshape.58
  8.1 0.1 fusion.4
  8.1 0.1 reduce_window_sum.11
  8.2 0.2 select_reduce_fusion
  8.4 1.6 reshape.59
  9.9 0.2 convolution_convert_fusion.5
  10.2 3.3 convolution_convert_fusion.1
  13.5 7.4 %reshape.60 = bf16[32,32,2048]{2,1,0:T(8,128)(2,1)} reshape(bf16[64,32768]{1,0:T(8,128)(2,1)} %convolution_convert_fusion.1) | data formatting | bytes 8388608 | tf_op jit(solution)/shard_map/reshape | solution.py:31
  20.9 0.0 copy-start.5
  20.9 60.3 %all_to_all.15 = bf16[32,32,2048]{2,1,0:T(8,128)(2,1)S(1)} all-to-all(bf16[32,32,2048]{2,1,0:T(8,128)(2,1)} %reshape.60), channel_id=1, replica_groups=mesh['dp'=4,'dict'=32] {'dict'}, dimensions={0} | all-to-all | bytes 8388608 | tf_op jit(solution)/shard_map/all_to_all | solution.py:32
  81.2 0.0 copy-start
  81.2 2.0 copy-done
  83.1 0.0 copy-done.5
  83.1 6.0 %fusion.10 = f32[1024,1024]{1,0:T(8,128)} fusion(bf16[1024,2048]{1,0:T(8,128)(2,1)S(1)} %bitcast.16, bf16[2048,1024]{1,0:T(8,128)(2,1)S(1)} %copy-done.5), kind=kOutput, calls=%fused_computation.29 | convolution fusion | flops 4294967296 | bytes 12582912 | tf_op jit(solution)/shard_map/dot_general | solution.py:34
  89.1 0.0 copy-start.4
  89.1 0.0 all-reduce.3.cloned.1.call-update
  89.1 0.7 copy-done.4
  89.8 89.8 %all-reduce.3.cloned.1.call-done = f32[1024,1024]{1,0:T(8,128)} async-done(((f32[1024,1024]{1,0:T(8,128)}), f32[1024,1024]{1,0:T(8,128)}) %all-reduce.3.cloned.1.call-update) | async-done | bytes 4194320 | tf_op jit(solution)/shard_map/psum | solution.py:36
  179.6 10.0 %convolution_convert_fusion.4 = bf16[1024,2048]{1,0:T(8,128)(2,1)} fusion(bf16[1024,2048]{1,0:T(8,128)(2,1)} %param.9, f32[1024,1024]{1,0:T(8,128)} %all-reduce.3.cloned.1.call-done, f32[1024]{0:T(1024)S(1)} %convert_element_type.44), kind=kOutput, calls=%fused_computation.7 | convolution fusion | flops 4301258752 | bytes 12587008 | tf_op jit(solution)/shard_map/dot_general | solution.py:38
  189.6 0.0 copy-start.3
  189.6 8.0 %all-to-all-start.1 = ((bf16[32,32,2048]{2,1,0:T(8,128)(2,1)}), bf16[32,32,2048]{2,1,0:T(8,128)(2,1)}, u32[]{:S(2)}, u32[]{:S(2)}) async-start(bf16[32,32,2048]{2,1,0:T(8,128)(2,1)} %bitcast.20), calls=%async_computation.1 | async-start | bytes 8388608 | tf_op jit(solution)/shard_map/all_to_all | solution.py:40
  197.6 0.0 all-reduce.5.cloned.1.call-start
  197.7 0.0 copy-done.3
  197.7 52.0 %all-to-all-done.1 = bf16[32,32,2048]{2,1,0:T(8,128)(2,1)} async-done(((bf16[32,32,2048]{2,1,0:T(8,128)(2,1)}), bf16[32,32,2048]{2,1,0:T(8,128)(2,1)}, u32[]{:S(2)}, u32[]{:S(2)}) %all-to-all-start.1) | async-done | bytes 4194336 | tf_op jit(solution)/shard_map/all_to_all | solution.py:40
  249.7 7.4 %reshape.63 = bf16[64,32768]{1,0:T(8,128)(2,1)} reshape(bf16[32,32,2048]{2,1,0:T(8,128)(2,1)} %all-to-all-done.1) | data formatting | bytes 8388608 | tf_op jit(solution)/shard_map/reshape | solution.py:41
  257.1 0.0 copy-start.2
  257.1 4.3 fusion.11
  261.4 1.7 reshape.64
  263.1 0.0 copy-done.2
  263.1 1.3 multiply_convert_fusion.3
  264.5 1.6 reshape.65
  266.0 3.3 convolution_convert_fusion
  269.3 7.4 %reshape.66 = bf16[32,32,2048]{2,1,0:T(8,128)(2,1)} reshape(bf16[64,32768]{1,0:T(8,128)(2,1)} %convolution_convert_fusion) | data formatting | bytes 8388608 | tf_op jit(solution)/shard_map/reshape | solution.py:52
  276.7 0.0 copy-start.6
  276.7 57.9 %all_to_all.16 = bf16[32,32,2048]{2,1,0:T(8,128)(2,1)S(1)} all-to-all(bf16[32,32,2048]{2,1,0:T(8,128)(2,1)} %reshape.66), channel_id=1, replica_groups=mesh['dp'=4,'dict'=32] {'dict'}, dimensions={0} | all-to-all | bytes 8388608 | tf_op jit(solution)/shard_map/all_to_all | solution.py:53
  334.6 0.0 copy-start.1
  334.6 1.9 copy-done.1
  336.5 0.0 copy-done.6
  336.5 6.1 %fusion.12 = f32[1024,1024]{1,0:T(8,128)} fusion(bf16[1024,2048]{1,0:T(8,128)(2,1)S(1)} %bitcast.18, bf16[1024,2048]{1,0:T(8,128)(2,1)S(1)} %copy-done.6), kind=kOutput, calls=%fused_computation.31 | convolution fusion | flops 4294967296 | bytes 12582912 | tf_op jit(solution)/shard_map/dot_general | solution.py:59
  342.6 0.0 all-reduce.5.cloned.1.call-update
  342.6 10.1 %convolution_convert_fusion.2 = bf16[1024,2048]{1,0:T(8,128)(2,1)} fusion(bf16[1024,2048]{1,0:T(8,128)(2,1)} %bitcast.19, f32[1024,1024]{1,0:T(8,128)} %all-reduce.3.cloned.1.call-done, f32[1024]{0:T(1024)S(1)} %convert_element_type.44), kind=kOutput, calls=%fused_computation.5 | convolution fusion | flops 4301258752 | bytes 12587008 | tf_op jit(solution)/shard_map/dot_general | solution.py:56
  352.7 78.8 %all-reduce.5.cloned.1.call-done = f32[1024,1024]{1,0:T(8,128)} async-done(((f32[1024,1024]{1,0:T(8,128)}), f32[1024,1024]{1,0:T(8,128)}) %all-reduce.5.cloned.1.call-update) | async-done | bytes 4194320 | tf_op jit(solution)/shard_map/psum | solution.py:62
  431.5 11.3 %convolution_convert_fusion.3 = bf16[2048,1024]{1,0:T(8,128)(2,1)} fusion(bf16[1024,2048]{1,0:T(8,128)(2,1)} %bitcast.17, f32[1024,1024]{1,0:T(8,128)} %all-reduce.5.cloned.1.call-done, f32[1024,1024]{1,0:T(8,128)} %all-reduce.3.cloned.1.call-done, f32[1024]{0:T(1024)S(1)} %convert_element_type.44), kind=kOutput, calls=%fused_computation.6 | convolution fusion | flops 4302307328 | bytes 16781312 | tf_op jit(solution)/shard_map/dot_general | solution.py:64
  (3 shorter events, 0.0 us)
Async XLA Ops:
  7.2 172.5 %all-reduce.3.cloned.1.call-start = ((), (), s32[]{:S(2)}) async-start(), calls=%async_computation.3 | async-start | bytes 8388608 | tf_op jit(solution)/shard_map/psum | solution.py:36
  20.9 62.3 %copy-start.5 = (bf16[2048,1024]{1,0:T(8,128)(2,1)S(1)}, bf16[2048,1024]{1,0:T(8,128)(2,1)}, u32[]{:S(2)}) copy-start(bf16[2048,1024]{1,0:T(8,128)(2,1)} %param.8) | copy-start | bytes 12582916
  81.2 2.0 copy-start
  89.1 0.7 copy-start.4
  189.6 8.1 %copy-start.3 = (bf16[2048]{0:T(1024)(128)(2,1)S(1)}, bf16[2048]{0:T(1024)(128)(2,1)}, u32[]{:S(2)}) copy-start(bf16[2048]{0:T(1024)(128)(2,1)} %param.11) | copy-start | bytes 12292
  189.6 60.1 %all-to-all-start.1 = ((bf16[32,32,2048]{2,1,0:T(8,128)(2,1)}), bf16[32,32,2048]{2,1,0:T(8,128)(2,1)}, u32[]{:S(2)}, u32[]{:S(2)}) async-start(bf16[32,32,2048]{2,1,0:T(8,128)(2,1)} %bitcast.20), calls=%async_computation.1 | async-start | bytes 8388608 | tf_op jit(solution)/shard_map/all_to_all | solution.py:40
  197.6 233.8 %all-reduce.5.cloned.1.call-start = ((), (), s32[]{:S(2)}) async-start(), calls=%async_computation.4 | async-start | bytes 8388608 | tf_op jit(solution)/shard_map/psum | solution.py:62
  257.1 6.0 %copy-start.2 = (bf16[256,2048]{1,0:T(8,128)(2,1)S(1)}, bf16[256,2048]{1,0:T(8,128)(2,1)}, u32[]{:S(2)}) copy-start(bf16[256,2048]{1,0:T(8,128)(2,1)} %param.6) | copy-start | bytes 3145732
  276.7 59.9 %copy-start.6 = (bf16[1024,2048]{1,0:T(8,128)(2,1)S(1)}, bf16[1024,2048]{1,0:T(8,128)(2,1)}, u32[]{:S(2)}) copy-start(bf16[1024,2048]{1,0:T(8,128)(2,1)} %param.9) | copy-start | bytes 12582916
  334.6 1.9 copy-start.1
Sparse Core Ops, SparseCore 0:
  89.3 90.3 all-reduce.2
  342.7 88.6 all-reduce.4
where the time goes:
time: 450 us
  waiting for transfers between devices  221 us (49%)
  blocking collectives  118 us (26%)
  matrix products  54.5 us (12%)
  local copies, waits for them, and re-layouts  32.4 us (7%)
  between operations  14.1 us (3%)
  starting transfers between devices  8.1 us (2%)
    psum x1, waiting for transfers between devices, on_device(): preact = lax.psum(pre_local, 'dp') + bias_enc  89.8 us
    psum x1, waiting for transfers between devices, on_device(): dact = lax.psum(dact_local, 'dp')  78.8 us
    all_to_all x1, blocking collectives, on_device(): lax.all_to_all(outgoing, 'dict', split_axis=0, concat_axis=0, tiled=True)  60.3 us
    all_to_all x1, blocking collectives, on_device(): lax.all_to_all(resid_out, 'dict', split_axis=0, concat_axis=0, tiled=True)  57.9 us
    all_to_all x1, waiting for transfers between devices, on_device(): lax.all_to_all(part, 'dict', split_axis=0, concat_axis=0, tiled=True)  52 us
    dot_general x1, matrix products, on_device(): lax.dot_general(rows_in, grad_pre, (((0,), (0,)), ((), ())), preferred_el...  11.3 us
    dot_general x1, matrix products, on_device(): lax.dot_general(activity, residual_in, (((0,), (0,)), ((), ())), preferre...  10.1 us
    dot_general x1, matrix products, on_device(): jnp.dot(activity, w_dec, preferred_element_type=jnp.float32)  9.98 us
  transfers between devices with their start and end apart: 3, of which 3 were waited for; matrix products, arithmetic and copies ran while one was open for 2% of the time, Pallas kernels for 0%

commit v1 on v0

--- a/solution.py
+++ b/solution.py
@@ -59,7 +59,9 @@
     dact_local = lax.dot_general(
         residual_in, w_dec, (((1,), (1,)), ((), ())), preferred_element_type=jnp.float32
     )
-    dact = lax.psum(dact_local, "dp")
+    dact = dact_local
+    for hop in (1, 2):
+        dact = dact + lax.ppermute(dact, "dp", [(dev, dev ^ hop) for dev in range(4)])
     grad_pre = (dact * 2.0 * jnp.maximum(preact, 0.0)).astype(jnp.bfloat16)
     grad_enc = lax.dot_general(
         rows_in, grad_pre, (((0,), (0,)), ((), ())), preferred_element_type=jnp.float32

time: 450 us -> 540 us (1.20)
  waiting for transfers between devices: 221 us -> 319 us
  matrix products: 54.5 us -> 44.3 us
    ppermute x0 -> x2, waiting for transfers between devices: none -> 177 us  [on_device(): lax.ppermute(dact, 'dp', [(dev, dev ^ hop) for dev in range(4)])]
    psum x1 -> x0, waiting for transfers between devices: 78.8 us -> none  [on_device(): dact = lax.psum(dact_local, 'dp')]
  transfers between devices with their start and end apart: 3 -> 4, of which waited for: 3 -> 4; matrix products, arithmetic and copies ran while one was open for 2% -> 1% of each run, Pallas kernels for 0% -> 0%
where the time goes in v1:
time: 540 us; the launch traced here: 538 us
  waiting for transfers between devices  319 us (59%)
  blocking collectives  118 us (22%)
  matrix products  44.3 us (8%)
  local copies, waits for them, and re-layouts  30.5 us (6%)
  between operations  14.1 us (3%)
  starting transfers between devices  9.61 us (2%)
    ppermute x2, waiting for transfers between devices, on_device(): lax.ppermute(dact, 'dp', [(dev, dev ^ hop) for dev in range(4)])  177 us
    psum x1, waiting for transfers between devices, on_device(): preact = lax.psum(pre_local, 'dp') + bias_enc  89.8 us
    all_to_all x1, blocking collectives, on_device(): lax.all_to_all(outgoing, 'dict', split_axis=0, concat_axis=0, tiled=True)  60.3 us
    all_to_all x1, blocking collectives, on_device(): lax.all_to_all(resid_out, 'dict', split_axis=0, concat_axis=0, tiled=True)  57.9 us
    all_to_all x1, waiting for transfers between devices, on_device(): lax.all_to_all(part, 'dict', split_axis=0, concat_axis=0, tiled=True)  52.1 us
  transfers between devices with their start and end apart: 4, of which 4 were waited for; matrix products, arithmetic and copies ran while one was open for 1% of the time, Pallas kernels for 0%

profile of v1, /device:TPU:1, one launch (start us, length us, event | category | flops | bytes accessed | tf_op | source)
XLA Modules:
  0.0 538.3 jit_solution(11361581139872615480)
XLA Ops:
  7.2 0.0 all-reduce.2.cloned.1.call-start
  7.2 0.8 copy.9
  8.0 0.1 reshape.58
  8.1 0.1 fusion.4
  8.1 0.1 reduce_window_sum.11
  8.2 0.2 select_reduce_fusion
  8.4 1.6 reshape.59
  9.9 0.2 convolution_convert_fusion.5
  10.2 3.3 convolution_convert_fusion.1
  13.5 7.4 %reshape.60 = bf16[32,32,2048]{2,1,0:T(8,128)(2,1)} reshape(bf16[64,32768]{1,0:T(8,128)(2,1)} %convolution_convert_fusion.1) | data formatting | bytes 8388608 | tf_op jit(solution)/shard_map/reshape | solution.py:31
  20.9 0.0 copy-start.5
  20.9 60.3 %all_to_all.15 = bf16[32,32,2048]{2,1,0:T(8,128)(2,1)S(1)} all-to-all(bf16[32,32,2048]{2,1,0:T(8,128)(2,1)} %reshape.60), channel_id=1, replica_groups=mesh['dp'=4,'dict'=32] {'dict'}, dimensions={0} | all-to-all | bytes 8388608 | tf_op jit(solution)/shard_map/all_to_all | solution.py:32
  81.2 0.0 copy-start
  81.2 2.0 copy-done
  83.2 0.0 copy-done.5
  83.2 6.0 %fusion.10 = f32[1024,1024]{1,0:T(8,128)} fusion(bf16[1024,2048]{1,0:T(8,128)(2,1)S(1)} %bitcast.16, bf16[2048,1024]{1,0:T(8,128)(2,1)S(1)} %copy-done.5), kind=kOutput, calls=%fused_computation.29 | convolution fusion | flops 4294967296 | bytes 12582912 | tf_op jit(solution)/shard_map/dot_general | solution.py:34
  89.2 0.0 copy-start.4
  89.2 0.0 all-reduce.2.cloned.1.call-update
  89.2 0.7 copy-done.4
  89.8 89.8 %all-reduce.2.cloned.1.call-done = f32[1024,1024]{1,0:T(8,128)} async-done(((f32[1024,1024]{1,0:T(8,128)}), f32[1024,1024]{1,0:T(8,128)}) %all-reduce.2.cloned.1.call-update) | async-done | bytes 4194320 | tf_op jit(solution)/shard_map/psum | solution.py:36
  179.7 10.0 %convolution_convert_fusion.4 = bf16[1024,2048]{1,0:T(8,128)(2,1)} fusion(bf16[1024,2048]{1,0:T(8,128)(2,1)} %param.9, f32[1024,1024]{1,0:T(8,128)} %all-reduce.2.cloned.1.call-done, f32[1024]{0:T(1024)S(1)} %convert_element_type.44), kind=kOutput, calls=%fused_computation.7 | convolution fusion | flops 4301258752 | bytes 12587008 | tf_op jit(solution)/shard_map/dot_general | solution.py:38
  189.6 0.0 copy-start.3
  189.6 8.0 %all-to-all-start.1 = ((bf16[32,32,2048]{2,1,0:T(8,128)(2,1)}), bf16[32,32,2048]{2,1,0:T(8,128)(2,1)}, u32[]{:S(2)}, u32[]{:S(2)}) async-start(bf16[32,32,2048]{2,1,0:T(8,128)(2,1)} %bitcast.20), calls=%async_computation.1 | async-start | bytes 8388608 | tf_op jit(solution)/shard_map/all_to_all | solution.py:40
  197.7 0.0 copy-done.3
  197.7 52.1 %all-to-all-done.1 = bf16[32,32,2048]{2,1,0:T(8,128)(2,1)} async-done(((bf16[32,32,2048]{2,1,0:T(8,128)(2,1)}), bf16[32,32,2048]{2,1,0:T(8,128)(2,1)}, u32[]{:S(2)}, u32[]{:S(2)}) %all-to-all-start.1) | async-done | bytes 4194336 | tf_op jit(solution)/shard_map/all_to_all | solution.py:40
  249.8 7.4 %reshape.63 = bf16[64,32768]{1,0:T(8,128)(2,1)} reshape(bf16[32,32,2048]{2,1,0:T(8,128)(2,1)} %all-to-all-done.1) | data formatting | bytes 8388608 | tf_op jit(solution)/shard_map/reshape | solution.py:41
  257.2 0.0 copy-start.2
  257.2 4.3 fusion.11
  261.4 1.7 reshape.64
  263.2 0.0 copy-done.2
  263.2 1.3 multiply_convert_fusion.3
  264.5 1.6 reshape.65
  266.1 3.3 convolution_convert_fusion
  269.4 7.4 %reshape.66 = bf16[32,32,2048]{2,1,0:T(8,128)(2,1)} reshape(bf16[64,32768]{1,0:T(8,128)(2,1)} %convolution_convert_fusion) | data formatting | bytes 8388608 | tf_op jit(solution)/shard_map/reshape | solution.py:52
  276.8 0.0 copy-start.6
  276.8 57.9 %all_to_all.16 = bf16[32,32,2048]{2,1,0:T(8,128)(2,1)S(1)} all-to-all(bf16[32,32,2048]{2,1,0:T(8,128)(2,1)} %reshape.66), channel_id=1, replica_groups=mesh['dp'=4,'dict'=32] {'dict'}, dimensions={0} | all-to-all | bytes 8388608 | tf_op jit(solution)/shard_map/all_to_all | solution.py:53
  334.7 0.0 copy-done.6
  334.7 4.5 fusion.12
  339.2 0.0 copy-start.7
  339.2 0.2 collective-permute-start
  339.4 91.9 %collective-permute-done = f32[1024,1024]{1,0:T(8,128)S(1)} collective-permute-done((f32[1024,1024]{1,0:T(8,128)S(1)}, f32[1024,1024]{1,0:T(8,128)S(1)}, u32[]{:S(2)}, u32[]{:S(2)}) %collective-permute-start) | collective-permute-done | bytes 4194336 | tf_op jit(solution)/shard_map/ppermute | solution.py:64
  431.3 1.0 add.42
  432.3 0.0 copy-start.1
  432.3 1.4 collective-permute-start.1
  433.7 0.0 copy-done.7
  433.7 6.3 %convolution_convert_fusion.2 = bf16[1024,2048]{1,0:T(8,128)(2,1)} fusion(bf16[1024,2048]{1,0:T(8,128)(2,1)S(1)} %bitcast.19, f32[1024,1024]{1,0:T(8,128)S(1)} %copy-done.7, f32[1024]{0:T(1024)S(1)} %convert_element_type.44), kind=kOutput, calls=%fused_computation.5 | convolution fusion | flops 4301258752 | bytes 12587008 | tf_op jit(solution)/shard_map/dot_general | solution.py:56
  440.0 85.1 %collective-permute-done.1 = f32[1024,1024]{1,0:T(8,128)S(1)} collective-permute-done((f32[1024,1024]{1,0:T(8,128)S(1)}, f32[1024,1024]{1,0:T(8,128)S(1)}, u32[]{:S(2)}, u32[]{:S(2)}) %collective-permute-start.1) | collective-permute-done | bytes 4194336 | tf_op jit(solution)/shard_map/ppermute | solution.py:64
  525.1 0.0 copy-done.1
  525.1 6.4 %convolution_convert_fusion.3 = bf16[2048,1024]{1,0:T(8,128)(2,1)} fusion(bf16[1024,2048]{1,0:T(8,128)(2,1)S(1)} %bitcast.17, f32[1024,1024]{1,0:T(8,128)S(1)} %add.42, f32[1024,1024]{1,0:T(8,128)S(1)} %collective-permute-done.1, f32[1024,1024]{1,0:T(8,128)S(1)} %copy-done.7, f32[1024]{0:T(1024)S(1)} %convert_element_type.44), kind=kOutput, calls=%fused_computation.6 | convolution fusion | flops 4303355904 | bytes 20975616 | tf_op jit(solution)/shard_map/dot_general | solution.py:66
  (3 shorter events, 0.0 us)
Async XLA Ops:
  7.2 172.5 %all-reduce.2.cloned.1.call-start = ((), (), s32[]{:S(2)}) async-start(), calls=%async_computation.3 | async-start | bytes 8388608 | tf_op jit(solution)/shard_map/psum | solution.py:36
  20.9 62.3 %copy-start.5 = (bf16[2048,1024]{1,0:T(8,128)(2,1)S(1)}, bf16[2048,1024]{1,0:T(8,128)(2,1)}, u32[]{:S(2)}) copy-start(bf16[2048,1024]{1,0:T(8,128)(2,1)} %param.8) | copy-start | bytes 12582916
  81.2 2.0 copy-start
  89.2 0.7 copy-start.4
  189.6 8.0 %copy-start.3 = (bf16[2048]{0:T(1024)(128)(2,1)S(1)}, bf16[2048]{0:T(1024)(128)(2,1)}, u32[]{:S(2)}) copy-start(bf16[2048]{0:T(1024)(128)(2,1)} %param.11) | copy-start | bytes 12292
  189.6 60.1 %all-to-all-start.1 = ((bf16[32,32,2048]{2,1,0:T(8,128)(2,1)}), bf16[32,32,2048]{2,1,0:T(8,128)(2,1)}, u32[]{:S(2)}, u32[]{:S(2)}) async-start(bf16[32,32,2048]{2,1,0:T(8,128)(2,1)} %bitcast.20), calls=%async_computation.1 | async-start | bytes 8388608 | tf_op jit(solution)/shard_map/all_to_all | solution.py:40
  257.2 6.0 %copy-start.2 = (bf16[256,2048]{1,0:T(8,128)(2,1)S(1)}, bf16[256,2048]{1,0:T(8,128)(2,1)}, u32[]{:S(2)}) copy-start(bf16[256,2048]{1,0:T(8,128)(2,1)} %param.6) | copy-start | bytes 3145732
  276.8 57.9 %copy-start.6 = (bf16[1024,2048]{1,0:T(8,128)(2,1)S(1)}, bf16[1024,2048]{1,0:T(8,128)(2,1)}, u32[]{:S(2)}) copy-start(bf16[1024,2048]{1,0:T(8,128)(2,1)} %param.9) | copy-start | bytes 12582916
  339.2 94.5 %copy-start.7 = (f32[1024,1024]{1,0:T(8,128)S(1)}, f32[1024,1024]{1,0:T(8,128)}, u32[]{:S(2)}) copy-start(f32[1024,1024]{1,0:T(8,128)} %all-reduce.2.cloned.1.call-done) | copy-start | bytes 12582916
  339.2 92.1 %collective-permute-start = (f32[1024,1024]{1,0:T(8,128)S(1)}, f32[1024,1024]{1,0:T(8,128)S(1)}, u32[]{:S(2)}, u32[]{:S(2)}) collective-permute-start(f32[1024,1024]{1,0:T(8,128)S(1)} %fusion.12), channel_id=1, source_target_pairs={{0,32},{32,0},{64,96},{96,64},{1,33},{33,1},{65,97},{97,65},{2,34}... | collective-permute-start | bytes 12582920 | tf_op jit(solution)/shard_map/ppermute | solution.py:64
  432.3 92.8 %copy-start.1 = (bf16[32,32,2048]{2,1,0:T(8,128)(2,1)S(1)}, bf16[32,32,2048]{2,1,0:T(8,128)(2,1)}, u32[]{:S(2)}) copy-start(bf16[32,32,2048]{2,1,0:T(8,128)(2,1)} %copy-done) | copy-start | bytes 12582916
  432.3 92.7 %collective-permute-start.1 = (f32[1024,1024]{1,0:T(8,128)S(1)}, f32[1024,1024]{1,0:T(8,128)S(1)}, u32[]{:S(2)}, u32[]{:S(2)}) collective-permute-start(f32[1024,1024]{1,0:T(8,128)S(1)} %add.42), channel_id=1, source_target_pairs={{0,64},{32,96},{64,0},{96,32},{1,65},{33,97},{65,1},{97,33},{2,66}... | collective-permute-start | bytes 12582920 | tf_op jit(solution)/shard_map/ppermute | solution.py:64
Sparse Core Ops, SparseCore 0:
  89.3 90.3 all-reduce.1
